TPU v7x, 32 devices: a whole 2x2x4 slice. The times are simulated.
32 devices in a mesh: fsdp: 32 (over z, y, x, core).
Axes of the slice: x: 2, y: 2, z: 4, core: 2. Of those that a mesh axis runs over, the one named last changes fastest.
Arguments:
- tokens: bfloat16 [2, 32, 576, 1024], P(None, 'fsdp'), may hold values from -5 to 5
- lengths: int32 [2, 32], P(None, 'fsdp'), may hold values from 196 to 576, as said below
- cotangent: float32 [2, 32, 8, 1024], P(None, 'fsdp'), may hold values from -768 to 768
- ln1_gain: bfloat16 [1024], P('fsdp'), may hold values from 0.5 to 1.5
- ln1_bias: bfloat16 [1024], P('fsdp'), may hold values from -1.1953125 to 1.1953125
- w_qkv: bfloat16 [1024, 3072], P('fsdp'), may hold values from -0.25 to 0.25
- b_qv: bfloat16 [2048], P('fsdp'), may hold values from -1.1953125 to 1.1953125
- w_out: bfloat16 [1024, 1024], P('fsdp'), may hold values from -0.375 to 0.375
- b_out: bfloat16 [1024], P('fsdp'), may hold values from -1.1953125 to 1.1953125
- ln2_gain: bfloat16 [1024], P('fsdp'), may hold values from 0.5 to 1.5
- ln2_bias: bfloat16 [1024], P('fsdp'), may hold values from -1.1953125 to 1.1953125
- w_up: bfloat16 [1024, 4096], P('fsdp'), may hold values from -0.1875 to 0.1875
- b_up: bfloat16 [4096], P('fsdp'), may hold values from -1.1953125 to 1.1953125
- w_down: bfloat16 [4096, 1024], P('fsdp'), may hold values from -0.09375 to 0.09375
- b_down: bfloat16 [1024], P('fsdp'), may hold values from -1.1953125 to 1.1953125
- ln3_gain: bfloat16 [1024], P('fsdp'), may hold values from 0.5 to 1.5
- ln3_bias: bfloat16 [1024], P('fsdp'), may hold values from -1.1953125 to 1.1953125
- w_learn: bfloat16 [1024, 1024], P('fsdp'), may hold values from -0.1875 to 0.1875
- b_learn: bfloat16 [1024], P('fsdp'), may hold values from -1.1953125 to 1.1953125
- w_map: bfloat16 [1024, 8], P('fsdp'), may hold values from -0.75 to 0.75
Outputs:
- pooled: float32 [2, 32, 8, 1024], P(None, 'fsdp')
- d_tokens: float32 [2, 32, 576, 1024], P(None, 'fsdp')
- grad_ln1_gain: float32 [1024], P('fsdp')
- grad_ln1_bias: float32 [1024], P('fsdp')
- grad_w_qkv: float32 [1024, 3072], P('fsdp')
- grad_b_qv: float32 [2048], P('fsdp')
- grad_w_out: float32 [1024, 1024], P('fsdp')
- grad_b_out: float32 [1024], P('fsdp')
- grad_ln2_gain: float32 [1024], P('fsdp')
- grad_ln2_bias: float32 [1024], P('fsdp')
- grad_w_up: float32 [1024, 4096], P('fsdp')
- grad_b_up: float32 [4096], P('fsdp')
- grad_w_down: float32 [4096, 1024], P('fsdp')
- grad_b_down: float32 [1024], P('fsdp')
- grad_ln3_gain: float32 [1024], P('fsdp')
- grad_ln3_bias: float32 [1024], P('fsdp')
- grad_w_learn: float32 [1024, 1024], P('fsdp')
- grad_b_learn: float32 [1024], P('fsdp')
- grad_w_map: float32 [1024, 8], P('fsdp')
Inputs may be any that keep to these rules, and one draw needn't show every extreme that they name: `lengths`: each image has 196 or 576 patches; both counts occur in every draw.
All inputs are finite; a program needn't handle non-finite values.
Results may differ from a plain program's by a relative error of at most 0.013.
Values may be sent and summed in bfloat16 or wider, within the bound.
No kernel may reach another device: no remote copies, remote signals or barrier semaphores. Data moves between devices by JAX's collectives and lax.ppermute only.
A program may use at most 448 MiB of HBM per device.

v0:
```python
import jax
import jax.numpy as jnp
from jax import lax
from jax.sharding import PartitionSpec as P

D = 1024
HEADS = 16
HD = 64
EPSILON = 1e-06
SCALE = 0.125


def layer_norm(values, gain, shift):
    row_mean = jnp.mean(values, axis=-1, keepdims=True)
    centered = values - row_mean
    variance = jnp.mean(centered * centered, axis=-1, keepdims=True)
    return centered * lax.rsqrt(variance + EPSILON) * gain + shift


def norm_back(values, gain, shift, incoming):
    _, pull_back = jax.vjp(layer_norm, values, gain, shift)
    return pull_back(incoming)


def gelu_exact(values):
    return jax.nn.gelu(values, approximate=False)


def gelu_slope(values, incoming):
    _, pull_back = jax.vjp(gelu_exact, values)
    return pull_back(incoming)[0]


def product(left, right):
    return jnp.dot(left, right, preferred_element_type=jnp.float32)


def product_rows(left, right):
    return lax.dot_general(
        left, right, (((0,), (0,)), ((), ())), preferred_element_type=jnp.float32
    )


def product_back(left, right):
    return lax.dot_general(
        left, right, (((1,), (1,)), ((), ())), preferred_element_type=jnp.float32
    )


def attention_scores(queries, key_rows, slot_valid):
    scores = (
        jnp.einsum("qhd,khd->hqk", queries, key_rows, preferred_element_type=jnp.float32) * SCALE
    )
    return jnp.where(slot_valid[None, None, :], scores, -1e30)


def unflatten_all(flat_local, grads, devices):
    pieces = []
    offset = 0
    for item in grads:
        local_shape = (item.shape[0] // devices,) + item.shape[1:]
        count = item.size // devices
        pieces.append(flat_local[offset : offset + count].reshape(local_shape))
        offset = offset + count
    return tuple(pieces)


def image_forward(params, image_rows, length):
    (
        ln1_gain,
        ln1_bias,
        w_qkv,
        b_qv,
        w_out,
        b_out,
        ln2_gain,
        ln2_bias,
        w_up,
        b_up,
        w_down,
        b_down,
        ln3_gain,
        ln3_bias,
        w_learn,
        b_learn,
        w_map,
    ) = params
    slot_count = image_rows.shape[0]
    slot_valid = lax.iota(jnp.int32, slot_count) < length
    source = image_rows.astype(jnp.float32)
    hidden = layer_norm(source, ln1_gain.astype(jnp.float32), ln1_bias.astype(jnp.float32)).astype(
        jnp.bfloat16
    )
    qkv_rows = product(hidden, w_qkv)
    qv_bias = b_qv.astype(jnp.float32)
    queries = (qkv_rows[:, :D] + qv_bias[:D]).astype(jnp.bfloat16).reshape(slot_count, HEADS, HD)
    key_rows = qkv_rows[:, D : 2 * D].astype(jnp.bfloat16).reshape(slot_count, HEADS, HD)
    values = (
        (qkv_rows[:, 2 * D :] + qv_bias[D:]).astype(jnp.bfloat16).reshape(slot_count, HEADS, HD)
    )
    scores = attention_scores(queries, key_rows, slot_valid)
    row_top = jnp.max(scores, axis=-1, keepdims=True)
    row_total = jnp.sum(jnp.exp(scores - row_top), axis=-1, keepdims=True)
    log_total = row_top + jnp.log(row_total)
    probs_low = jnp.exp(scores - log_total).astype(jnp.bfloat16)
    attended = jnp.einsum("hqk,khd->qhd", probs_low, values, preferred_element_type=jnp.float32)
    attended = attended.reshape(slot_count, D).astype(jnp.bfloat16)
    middle = source + product(attended, w_out) + b_out.astype(jnp.float32)
    normed = layer_norm(middle, ln2_gain.astype(jnp.float32), ln2_bias.astype(jnp.float32)).astype(
        jnp.bfloat16
    )
    up_proj = product(normed, w_up) + b_up.astype(jnp.float32)
    up_act = gelu_exact(up_proj).astype(jnp.bfloat16)
    output = middle + product(up_act, w_down) + b_down.astype(jnp.float32)
    learn_in = layer_norm(
        output, ln3_gain.astype(jnp.float32), ln3_bias.astype(jnp.float32)
    ).astype(jnp.bfloat16)
    learn_mid = product(learn_in, w_learn) + b_learn.astype(jnp.float32)
    learn_act = gelu_exact(learn_mid).astype(jnp.bfloat16)
    logits = product(learn_act, w_map)
    pool_share = slot_valid.astype(jnp.float32) / length.astype(jnp.float32)
    pool_maps = jax.nn.sigmoid(logits) * pool_share[:, None]
    pooled = jnp.einsum("sm,sd->md", pool_maps, output, precision=lax.Precision.HIGHEST)
    saved = (
        queries,
        key_rows,
        values,
        log_total,
        attended,
        middle,
        normed,
        up_proj,
        up_act,
        output,
        learn_in,
        learn_mid,
        learn_act,
        logits,
    )
    return (pooled, saved)


def image_backward(params, image_rows, length, pool_grad, saved):
    (
        ln1_gain,
        ln1_bias,
        w_qkv,
        b_qv,
        w_out,
        b_out,
        ln2_gain,
        ln2_bias,
        w_up,
        b_up,
        w_down,
        b_down,
        ln3_gain,
        ln3_bias,
        w_learn,
        b_learn,
        w_map,
    ) = params
    (
        queries,
        key_rows,
        values,
        log_total,
        attended,
        middle,
        normed,
        up_proj,
        up_act,
        output,
        learn_in,
        learn_mid,
        learn_act,
        logits,
    ) = saved
    slot_count = image_rows.shape[0]
    slot_valid = lax.iota(jnp.int32, slot_count) < length
    source = image_rows.astype(jnp.float32)
    pool_share = slot_valid.astype(jnp.float32) / length.astype(jnp.float32)
    squashed = jax.nn.sigmoid(logits)
    pool_maps = squashed * pool_share[:, None]
    d_maps = jnp.einsum("sd,md->sm", output, pool_grad, precision=lax.Precision.HIGHEST)
    d_logits = (d_maps * pool_share[:, None] * squashed * (1.0 - squashed)).astype(jnp.bfloat16)
    d_output = jnp.einsum("sm,md->sd", pool_maps, pool_grad, precision=lax.Precision.HIGHEST)
    g_map = product_rows(learn_act, d_logits)
    d_learn = gelu_slope(learn_mid, product_back(d_logits, w_map)).astype(jnp.bfloat16)
    g_blearn = jnp.sum(d_learn.astype(jnp.float32), axis=0)
    g_wlearn = product_rows(learn_in, d_learn)
    d_norm3, g_ln3, h_ln3 = norm_back(
        output,
        ln3_gain.astype(jnp.float32),
        ln3_bias.astype(jnp.float32),
        product_back(d_learn, w_learn),
    )
    d_output = d_output + d_norm3
    d_mlp = d_output.astype(jnp.bfloat16)
    g_bdown = jnp.sum(d_mlp.astype(jnp.float32), axis=0)
    g_wdown = product_rows(up_act, d_mlp)
    d_up = gelu_slope(up_proj, product_back(d_mlp, w_down)).astype(jnp.bfloat16)
    g_bup = jnp.sum(d_up.astype(jnp.float32), axis=0)
    g_wup = product_rows(normed, d_up)
    d_norm2, g_ln2, h_ln2 = norm_back(
        middle, ln2_gain.astype(jnp.float32), ln2_bias.astype(jnp.float32), product_back(d_up, w_up)
    )
    d_middle = d_output + d_norm2
    d_branch = d_middle.astype(jnp.bfloat16)
    g_bout = jnp.sum(d_branch.astype(jnp.float32), axis=0)
    g_wout = product_rows(attended, d_branch)
    d_attn = product_back(d_branch, w_out).astype(jnp.bfloat16).reshape(slot_count, HEADS, HD)
    scores = attention_scores(queries, key_rows, slot_valid)
    probs = jnp.exp(scores - log_total)
    probs_low = probs.astype(jnp.bfloat16)
    d_values = jnp.einsum(
        "hqk,qhd->khd", probs_low, d_attn, preferred_element_type=jnp.float32
    ).astype(jnp.bfloat16)
    d_probs = jnp.einsum("qhd,khd->hqk", d_attn, values, preferred_element_type=jnp.float32)
    d_scores = (probs * (d_probs - jnp.sum(probs * d_probs, axis=-1, keepdims=True))).astype(
        jnp.bfloat16
    )
    d_queries = (
        jnp.einsum("hqk,khd->qhd", d_scores, key_rows, preferred_element_type=jnp.float32) * SCALE
    ).astype(jnp.bfloat16)
    d_keys = (
        jnp.einsum("hqk,qhd->khd", d_scores, queries, preferred_element_type=jnp.float32) * SCALE
    ).astype(jnp.bfloat16)
    d_qkv = jnp.concatenate(
        [
            d_queries.reshape(slot_count, D),
            d_keys.reshape(slot_count, D),
            d_values.reshape(slot_count, D),
        ],
        axis=1,
    )
    g_bqv = jnp.concatenate(
        [
            jnp.sum(d_queries.reshape(slot_count, D).astype(jnp.float32), axis=0),
            jnp.sum(d_values.reshape(slot_count, D).astype(jnp.float32), axis=0),
        ]
    )
    gain_one = ln1_gain.astype(jnp.float32)
    bias_one = ln1_bias.astype(jnp.float32)
    hidden = layer_norm(source, gain_one, bias_one).astype(jnp.bfloat16)
    g_wqkv = product_rows(hidden, d_qkv)
    d_norm1, g_ln1, h_ln1 = norm_back(source, gain_one, bias_one, product_back(d_qkv, w_qkv))
    d_image = d_middle + d_norm1
    grad_parts = (
        g_ln1,
        h_ln1,
        g_wqkv,
        g_bqv,
        g_wout,
        g_bout,
        g_ln2,
        h_ln2,
        g_wup,
        g_bup,
        g_wdown,
        g_bdown,
        g_ln3,
        h_ln3,
        g_wlearn,
        g_blearn,
        g_map,
    )
    return (d_image, grad_parts)


def body(
    tokens,
    lengths,
    cotangent,
    ln1_gain,
    ln1_bias,
    w_qkv,
    b_qv,
    w_out,
    b_out,
    ln2_gain,
    ln2_bias,
    w_up,
    b_up,
    w_down,
    b_down,
    ln3_gain,
    ln3_bias,
    w_learn,
    b_learn,
    w_map,
):
    shards = (
        ln1_gain,
        ln1_bias,
        w_qkv,
        b_qv,
        w_out,
        b_out,
        ln2_gain,
        ln2_bias,
        w_up,
        b_up,
        w_down,
        b_down,
        ln3_gain,
        ln3_bias,
        w_learn,
        b_learn,
        w_map,
    )
    devices = lax.axis_size("fsdp")
    micro_count = tokens.shape[0]
    pooled_parts = []
    grad_image_parts = []
    grad_total = None
    for micro_step in range(micro_count):
        forward_params = (
            lax.all_gather(shards[0], "fsdp", axis=0, tiled=True),
            lax.all_gather(shards[1], "fsdp", axis=0, tiled=True),
            lax.all_gather(shards[2], "fsdp", axis=0, tiled=True),
            lax.all_gather(shards[3], "fsdp", axis=0, tiled=True),
            lax.all_gather(shards[4], "fsdp", axis=0, tiled=True),
            lax.all_gather(shards[5], "fsdp", axis=0, tiled=True),
            lax.all_gather(shards[6], "fsdp", axis=0, tiled=True),
            lax.all_gather(shards[7], "fsdp", axis=0, tiled=True),
            lax.all_gather(shards[8], "fsdp", axis=0, tiled=True),
            lax.all_gather(shards[9], "fsdp", axis=0, tiled=True),
            lax.all_gather(shards[10], "fsdp", axis=0, tiled=True),
            lax.all_gather(shards[11], "fsdp", axis=0, tiled=True),
            lax.all_gather(shards[12], "fsdp", axis=0, tiled=True),
            lax.all_gather(shards[13], "fsdp", axis=0, tiled=True),
            lax.all_gather(shards[14], "fsdp", axis=0, tiled=True),
            lax.all_gather(shards[15], "fsdp", axis=0, tiled=True),
            lax.all_gather(shards[16], "fsdp", axis=0, tiled=True),
        )

        def forward_one(item_pack):
            return image_forward(forward_params, item_pack[0], item_pack[1])

        pooled, saved = lax.map(forward_one, (tokens[micro_step], lengths[micro_step]))
        backward_params = (
            lax.all_gather(shards[0], "fsdp", axis=0, tiled=True),
            lax.all_gather(shards[1], "fsdp", axis=0, tiled=True),
            lax.all_gather(shards[2], "fsdp", axis=0, tiled=True),
            lax.all_gather(shards[3], "fsdp", axis=0, tiled=True),
            lax.all_gather(shards[4], "fsdp", axis=0, tiled=True),
            lax.all_gather(shards[5], "fsdp", axis=0, tiled=True),
            lax.all_gather(shards[6], "fsdp", axis=0, tiled=True),
            lax.all_gather(shards[7], "fsdp", axis=0, tiled=True),
            lax.all_gather(shards[8], "fsdp", axis=0, tiled=True),
            lax.all_gather(shards[9], "fsdp", axis=0, tiled=True),
            lax.all_gather(shards[10], "fsdp", axis=0, tiled=True),
            lax.all_gather(shards[11], "fsdp", axis=0, tiled=True),
            lax.all_gather(shards[12], "fsdp", axis=0, tiled=True),
            lax.all_gather(shards[13], "fsdp", axis=0, tiled=True),
            lax.all_gather(shards[14], "fsdp", axis=0, tiled=True),
            lax.all_gather(shards[15], "fsdp", axis=0, tiled=True),
            lax.all_gather(shards[16], "fsdp", axis=0, tiled=True),
        )
        grad_zero = tuple((jnp.zeros(item.shape, jnp.float32) for item in backward_params))

        def backward_one(grad_carry, item_pack):
            d_image, grad_parts = image_backward(
                backward_params, item_pack[0], item_pack[1], item_pack[2], item_pack[3]
            )
            return (tuple((left + right for left, right in zip(grad_carry, grad_parts))), d_image)

        micro_grads, d_images = lax.scan(
            backward_one,
            grad_zero,
            (tokens[micro_step], lengths[micro_step], cotangent[micro_step], saved),
        )
        if grad_total is None:
            grad_total = micro_grads
        else:
            grad_total = tuple((left + right for left, right in zip(grad_total, micro_grads)))
        pooled_parts.append(pooled)
        grad_image_parts.append(d_images)
    flat_terms = jnp.concatenate([item.reshape(devices, -1) for item in grad_total], axis=1)
    summed = lax.psum_scatter(flat_terms.reshape(-1), "fsdp", scatter_dimension=0, tiled=True)
    grad_total = unflatten_all(summed, grad_total, devices)
    return (jnp.stack(pooled_parts), jnp.stack(grad_image_parts)) + tuple(grad_total)


def solution(mesh):
    placed = (
        P(None, "fsdp", None, None),
        P(None, "fsdp"),
        P(None, "fsdp", None, None),
        P("fsdp"),
        P("fsdp"),
        P("fsdp", None),
        P("fsdp"),
        P("fsdp", None),
        P("fsdp"),
        P("fsdp"),
        P("fsdp"),
        P("fsdp", None),
        P("fsdp"),
        P("fsdp", None),
        P("fsdp"),
        P("fsdp"),
        P("fsdp"),
        P("fsdp", None),
        P("fsdp"),
        P("fsdp", None),
    )
    return jax.shard_map(
        body,
        mesh=mesh,
        in_specs=placed,
        out_specs=(
            P(None, "fsdp", None, None),
            P(None, "fsdp", None, None),
            P("fsdp"),
            P("fsdp"),
            P("fsdp", None),
            P("fsdp"),
            P("fsdp", None),
            P("fsdp"),
            P("fsdp"),
            P("fsdp"),
            P("fsdp", None),
            P("fsdp"),
            P("fsdp", None),
            P("fsdp"),
            P("fsdp"),
            P("fsdp"),
            P("fsdp", None),
            P("fsdp"),
            P("fsdp", None),
        ),
        check_vma=False,
    )
```

profile of v0, /device:TPU:0, one launch (start us, length us, event | category | flops | bytes accessed | tf_op | source)
XLA Modules:
  0.0 1819.9 jit_solution(6046457286659416338)
XLA Ops:
  26.6 42.9 %all-reduce.11 = (bf16[2048]{0:T(1024)(128)(2,1)S(1)}, bf16[1024]{0:T(1024)(128)(2,1)S(1)}, bf16[1024]{0:T(1024)(128)(2,1)S(1)}, bf16[1024]{0:T(1024)(128)(2,1)S...) all-reduce(bf16[2048]{0:T(1024)(128)(2,1)S(1)} %dynamic-update-slic, ...), channel_id=1, replica_groups=mesh['fsdp'=32] {'fsdp'}, use_global_device_ids=true, to_apply=%add.2 | all-reduce | flops 11264 | bytes 45056
  76.5 40.1 %all-gather = bf16[32,1,128]{2,1,0:T(2,128)(2,1)S(1)} all-gather(bf16[1,1,128]{2,1,0:T(2,128)(2,1)S(1)} %bitcast.258), channel_id=1, replica_groups=mesh['fsdp'=32] {'fsdp'}, dimensions={0}, use_global_device_ids=true | all-gather | bytes 8448 | tf_op jit(solution)/shard_map/all_gather | solution.py:328
  117.3 37.0 %all-gather.1 = bf16[32,32,8]{1,2,0:T(8,128)(2,1)S(1)} all-gather(bf16[1,32,8]{1,2,0:T(8,128)(2,1)S(1)} %bitcast.257), channel_id=1, replica_groups=mesh['fsdp'=32] {'fsdp'}, dimensions={0}, use_global_device_ids=true | all-gather | bytes 16896 | tf_op jit(solution)/shard_map/all_gather | solution.py:335
  187.0 14.6 fusion
  288.6 53.1 %multiply_convert_fusion.3 = (bf16[576,4096]{1,0:T(8,128)(2,1)}, f32[576,4096]{1,0:T(8,128)}, bf16[576,4096]{1,0:T(8,128)(2,1)}, f32[576,4096]{1,0:T(8,128)}, f32[576,4096]{1,0:T(8,128)}) fusion(f32[4096]{0:T(1024)S(1)} %bitcast.254, f32[576,4096]{1,0:T(8,128)S(1)} %fusion.126, bf16[1024,4096]{1,0:T(8,128)(2,1)S(1)} %copy-done.133, ...), kind=kOutput, calls=%fused_computation.35 | convolution fusion | flops 5146214400 | bytes 57963008 | tf_op jit(solution)/shard_map/while/body/eval_jaxpr/dot_general | solution.py:35
  410.6 17.2 convert_reduce_fusion.1
  427.8 13.0 fusion.122
  453.1 17.3 convert_reduce_fusion
  470.5 14.1 multiply_reduce_fusion.4
  505.8 16.8 multiply_reduce_fusion
  522.6 20.2 %multiply_convert_fusion = bf16[16,576,576]{1,2,0:T(8,128)(2,1)} fusion(f32[16,576,576]{1,2,0:T(8,128)} %get-tuple-element.659, f32[16,576,576]{1,2,0:T(8,128)} %get-tuple-element.595, f32[16,576]{1,0:T(8,128)S(1)} %get-tuple-element.658, f32[16,576]{1,0:T(8,128)S(1)} %copy-done.56, pred[576]{0:T(1024)(128)(4,1)S(1)} %copy-done.101), kind=kLoop, calls=%fused_computation | loop fusion | flops 31850496 | bytes 53158464 | tf_op jit(solution)/shard_map/while/body/eval_jaxpr/convert_element_type | solution.py:220
  577.6 16.2 multiply_reduce_fusion.1
  593.8 20.7 %multiply_convert_fusion.1 = bf16[16,576,576]{1,2,0:T(8,128)(2,1)} fusion(f32[16,576,576]{1,2,0:T(8,128)} %get-tuple-element.657, f32[16,576,576]{1,2,0:T(8,128)} %get-tuple-element.597, f32[16,576]{1,0:T(8,128)S(1)} %get-tuple-element.656, f32[16,576]{1,0:T(8,128)S(1)} %copy-done.54, pred[576]{0:T(1024)(128)(4,1)S(1)} %copy-done.99), kind=kLoop, calls=%fused_computation.2 | loop fusion | flops 31850496 | bytes 53158464 | tf_op jit(solution)/shard_map/while/body/eval_jaxpr/convert_element_type | solution.py:220
  656.0 15.2 convolution_add_fusion
  671.2 12.4 reshape.578
  683.6 15.0 convolution_add_fusion.1
  698.6 12.4 reshape.579
  748.3 15.8 convolution_add_fusion.2
  777.0 37.1 %dynamic-update-slice.12 = f32[32,426720]{1,0:T(8,128)} dynamic-update-slice(f32[32,426720]{1,0:T(8,128)} %dynamic-update-slice.11, f32[32,98304]{1,0:T(8,128)} %reshape.576, s32[]{} %constant.650, s32[]{} %constant.652) | dynamic-update-slice | bytes 25165828
  824.4 48.2 %dynamic-update-slice.18 = f32[32,426720]{1,0:T(8,128)} dynamic-update-slice(f32[32,426720]{1,0:T(8,128)} %dynamic-update-slice.17, f32[32,131072]{1,0:T(8,128)} %reshape.578, s32[]{} %constant.650, s32[]{} %constant.658) | dynamic-update-slice | bytes 33554436
  874.1 48.2 %dynamic-update-slice.20 = f32[32,426720]{1,0:T(8,128)} dynamic-update-slice(f32[32,426720]{1,0:T(8,128)} %dynamic-update-slice.19, f32[32,131072]{1,0:T(8,128)} %reshape.579, s32[]{} %constant.650, s32[]{} %constant.660) | dynamic-update-slice | bytes 33554436
  926.6 14.3 dynamic-update-slice.24
  944.1 77.3 %reshape.582 = f32[13655040]{0:T(1024)} reshape(f32[32,426720]{1,0:T(8,128)} %dynamic-update-slice.26) | data formatting | bytes 109240320 | tf_op jit(solution)/shard_map/reshape | solution.py:381
  1031.8 767.8 %all-reduce.14.cloned.1.call-done = f32[13655040]{0:T(1024)} async-done(((f32[13655040]{0:T(1024)}), f32[13655040]{0:T(1024)}) %all-reduce.14.cloned.1.call-update) | async-done | bytes 54620176
  (505 shorter events, 415.9 us)
Async XLA Ops:
  7.2 67.9 %copy-start.4 = (bf16[2,1,576,1024]{3,2,1,0:T(8,128)(2,1)S(1)}, bf16[2,1,576,1024]{3,2,1,0:T(8,128)(2,1)}, u32[]{:S(2)}) copy-start(bf16[2,1,576,1024]{3,2,1,0:T(8,128)(2,1)} %param.20) | copy-start | bytes 7077892
  7.2 147.9 %all-gather.8.cloned.1.call-start = ((), (), s32[]{:S(2)}) async-start(), calls=%async_computation | async-start | bytes 6488064 | tf_op jit(solution)/shard_map/all_gather | solution.py:321
  7.9 222.9 %all-gather.10.cloned.1.call-start = ((), (), s32[]{:S(2)}) async-start(), calls=%async_computation.1 | async-start | bytes 2162688 | tf_op jit(solution)/shard_map/all_gather | solution.py:323
  8.7 267.7 %all-gather.12.cloned.1.call-start = ((), (), s32[]{:S(2)}) async-start(), calls=%async_computation.2 | async-start | bytes 8650752 | tf_op jit(solution)/shard_map/all_gather | solution.py:327
  9.4 332.2 %all-gather.14.cloned.1.call-start = ((), (), s32[]{:S(2)}) async-start(), calls=%async_computation.3 | async-start | bytes 8650752 | tf_op jit(solution)/shard_map/all_gather | solution.py:329
  10.0 351.3 %all-gather.16.cloned.1.call-start = ((), (), s32[]{:S(2)}) async-start(), calls=%async_computation.4 | async-start | bytes 2162688 | tf_op jit(solution)/shard_map/all_gather | solution.py:333
  10.6 1789.0 %all-reduce.14.cloned.1.call-start = ((), (), s32[]{:S(2)}) async-start(), calls=%async_computation.5 | async-start | bytes 109240320
  69.4 96.3 %copy-start.76 = (f32[1024]{0:T(1024)}, f32[1024]{0:T(1024)S(1)}, u32[]{:S(2)}) copy-start(f32[1024]{0:T(1024)S(1)} %convert_element_type.370) | copy-start | bytes 12292
  70.0 85.1 %copy-start.124 = (f32[1024]{0:T(1024)}, f32[1024]{0:T(1024)S(1)}, u32[]{:S(2)}) copy-start(f32[1024]{0:T(1024)S(1)} %convert_element_type.371) | copy-start | bytes 12292
  70.0 357.7 %copy-start.57 = (f32[1024]{0:T(1024)}, f32[1024]{0:T(1024)S(1)}, u32[]{:S(2)}) copy-start(f32[1024]{0:T(1024)S(1)} %convert_element_type.382) | copy-start | bytes 12292
  73.0 44.3 %copy-start.131 = (bf16[32,8]{0,1:T(8,128)(2,1)S(1)}, bf16[32,8]{0,1:T(8,128)(2,1)}, u32[]{:S(2)}) copy-start(bf16[32,8]{0,1:T(8,128)(2,1)} %param.39) | copy-start | bytes 1540
  75.1 80.0 %copy-start.66 = (f32[576]{0:T(1024)}, f32[576]{0:T(1024)S(1)}, u32[]{:S(2)}) copy-start(f32[576]{0:T(1024)S(1)} %get-tuple-element.677) | copy-start | bytes 6916
  75.1 90.6 %copy-start.68 = (f32[576]{0:T(1024)}, f32[576]{0:T(1024)S(1)}, u32[]{:S(2)}) copy-start(f32[576]{0:T(1024)S(1)} %get-tuple-element.678) | copy-start | bytes 6916
  76.5 78.6 %copy-start.78 = (f32[576]{0:T(1024)}, f32[576]{0:T(1024)S(1)}, u32[]{:S(2)}) copy-start(f32[576]{0:T(1024)S(1)} %fusion.96) | copy-start | bytes 6916
  288.6 53.1 %copy-start.129 = (f32[1024]{0:T(1024)S(1)}, f32[1024]{0:T(1024)}, u32[]{:S(2)}) copy-start(f32[1024]{0:T(1024)} %convert_element_type.386) | copy-start | bytes 12292
  351.7 44.3 %copy-start.6 = (f32[576,1024]{1,0:T(8,128)}, f32[576,1024]{1,0:T(8,128)S(1)}, u32[]{:S(2)}) copy-start(f32[576,1024]{1,0:T(8,128)S(1)} %get-tuple-element.650) | copy-start | bytes 7077892
  359.4 36.5 %copy-start.93 = (f32[576]{0:T(1024)}, f32[576]{0:T(1024)S(1)}, u32[]{:S(2)}) copy-start(f32[576]{0:T(1024)S(1)} %broadcast_multiply_fusion) | copy-start | bytes 6916
  361.2 34.7 %copy-start.111 = (f32[576]{0:T(1024)}, f32[576]{0:T(1024)S(1)}, u32[]{:S(2)}) copy-start(f32[576]{0:T(1024)S(1)} %fusion.98) | copy-start | bytes 6916
  381.3 59.5 %copy-start.61 = (f32[576,8]{0,1:T(8,128)}, f32[576,8]{0,1:T(8,128)S(1)}, u32[]{:S(2)}) copy-start(f32[576,8]{0,1:T(8,128)S(1)} %fusion.65) | copy-start | bytes 55300
  400.3 160.1 %copy-start.14 = (f32[576,1024]{1,0:T(8,128)}, f32[576,1024]{1,0:T(8,128)S(1)}, u32[]{:S(2)}) copy-start(f32[576,1024]{1,0:T(8,128)S(1)} %add_add_fusion.9) | copy-start | bytes 7077892
  443.1 47.1 %copy-start.11 = (f32[576,1024]{1,0:T(8,128)}, f32[576,1024]{1,0:T(8,128)S(1)}, u32[]{:S(2)}) copy-start(f32[576,1024]{1,0:T(8,128)S(1)} %add_add_fusion.7) | copy-start | bytes 7077892
  777.0 37.1 %copy-start.95 = (f32[16,64]{1,0:T(8,128)S(1)}, f32[16,64]{1,0:T(8,128)}, u32[]{:S(2)}) copy-start(f32[16,64]{1,0:T(8,128)} %get-tuple-element.667) | copy-start | bytes 12292
  777.0 37.1 %copy-start.96 = (f32[16,64]{1,0:T(8,128)S(1)}, f32[16,64]{1,0:T(8,128)}, u32[]{:S(2)}) copy-start(f32[16,64]{1,0:T(8,128)} %get-tuple-element.665) | copy-start | bytes 12292
  777.0 37.1 %copy-start.97 = (f32[16,64]{1,0:T(8,128)S(1)}, f32[16,64]{1,0:T(8,128)}, u32[]{:S(2)}) copy-start(f32[16,64]{1,0:T(8,128)} %get-tuple-element.661) | copy-start | bytes 12292
  (130 other events, 922.0 us)
Sparse Core Ops, SparseCore 0:
  10.9 73.0 all-gather.7
  86.8 54.9 all-gather.9
  144.7 76.3 all-gather.11
  223.8 76.0 all-gather.13
  302.6 55.0 all-gather.15
  1021.6 777.9 all-reduce.13
where the time goes:
time: 1830 us; the launch traced here: 1820 us
  waiting for transfers between devices  771 us (42%)
  matrix products  433 us (24%)
  local copies, waits for them, and re-layouts  363 us (20%)
  blocking collectives  120 us (7%)
  other arithmetic  116 us (6%)
    unnamed x7, waiting for transfers between devices  771 us
    unnamed x334, local copies, waits for them, and re-layouts  207 us
    dot_general x12, matrix products, product(): return jnp.dot(left, right, preferred_element_type=jnp.float32)  112 us
    dot_general x12, matrix products, product_rows(): lax.dot_general(left, right, (((0,), (0,)), ((), ())), preferred_element_...  103 us
    dot_general x12, matrix products, product_back(): lax.dot_general(left, right, (((1,), (1,)), ((), ())), preferred_element_...  83.8 us
    reshape x1, local copies, waits for them, and re-layouts, body(): flat_terms.reshape(-1)  77.3 us
    reshape x6, local copies, waits for them, and re-layouts, body(): item.reshape(devices, -1)  45.1 us
    unnamed x1, blocking collectives  42.9 us
  transfers between devices with their start and end apart: 6, of which 1 were waited for; matrix products, arithmetic and copies ran while one was open for 12% of the time, Pallas kernels for 0%

commit v1 on v0

--- a/solution.py
+++ b/solution.py
@@ -315,6 +315,30 @@
     grad_image_parts = []
     grad_total = None
     for micro_step in range(micro_count):
+
+        def guide_the_files(v0):
+            response, tmp, current_value = (
+                lax.axis_size("fsdp"),
+                lax.axis_index("fsdp"),
+                v0.shape[0],
+            )
+            block_last, block_next = (v0, 1)
+            while block_next < response:
+                block_last = jnp.concatenate(
+                    [
+                        block_last,
+                        lax.ppermute(
+                            block_last,
+                            axis_name="fsdp",
+                            perm=tuple(((s, (s - block_next) % response) for s in range(response))),
+                        ),
+                    ],
+                    axis=0,
+                )
+                block_next = 2 * block_next
+            built = jnp.roll(block_last, shift=tmp * current_value, axis=0)
+            return built
+
         forward_params = (
             lax.all_gather(shards[0], "fsdp", axis=0, tiled=True),
             lax.all_gather(shards[1], "fsdp", axis=0, tiled=True),
@@ -325,7 +349,7 @@
             lax.all_gather(shards[6], "fsdp", axis=0, tiled=True),
             lax.all_gather(shards[7], "fsdp", axis=0, tiled=True),
             lax.all_gather(shards[8], "fsdp", axis=0, tiled=True),
-            lax.all_gather(shards[9], "fsdp", axis=0, tiled=True),
+            guide_the_files(shards[9]),
             lax.all_gather(shards[10], "fsdp", axis=0, tiled=True),
             lax.all_gather(shards[11], "fsdp", axis=0, tiled=True),
             lax.all_gather(shards[12], "fsdp", axis=0, tiled=True),

time: 1830 us -> 1830 us (level)
  blocking collectives: 120 us -> 82.2 us
    all_gather x1 -> x0, blocking collectives: 40.1 us -> none  [body(): lax.all_gather(shards[9], 'fsdp', axis=0, tiled=True)]
    unnamed x334 -> x344, local copies, waits for them, and re-layouts: 207 us -> 210 us
  transfers between devices with their start and end apart: 6 -> 11, of which waited for: 1 -> 4; matrix products, arithmetic and copies ran while one was open for 12% -> 12% of each run, Pallas kernels for 0% -> 0%
where the time goes in v1:
time: 1830 us; the launch traced here: 1820 us
  waiting for transfers between devices  787 us (43%)
  matrix products  433 us (24%)
  local copies, waits for them, and re-layouts  366 us (20%)
  other arithmetic  115 us (6%)
  blocking collectives  82.2 us (4%)
    unnamed x7, waiting for transfers between devices  770 us
    unnamed x344, local copies, waits for them, and re-layouts  210 us
    dot_general x12, matrix products, product(): return jnp.dot(left, right, preferred_element_type=jnp.float32)  111 us
    dot_general x12, matrix products, product_rows(): lax.dot_general(left, right, (((0,), (0,)), ((), ())), preferred_element_...  103 us
    dot_general x12, matrix products, product_back(): lax.dot_general(left, right, (((1,), (1,)), ((), ())), preferred_element_...  83.8 us
    reshape x1, local copies, waits for them, and re-layouts, body(): flat_terms.reshape(-1)  77.3 us
    reshape x6, local copies, waits for them, and re-layouts, body(): item.reshape(devices, -1)  45.2 us
    all_gather x1, blocking collectives, body(): lax.all_gather(shards[16], 'fsdp', axis=0, tiled=True)  44.6 us
  transfers between devices with their start and end apart: 11, of which 4 were waited for; matrix products, arithmetic and copies ran while one was open for 12% of the time, Pallas kernels for 0%

profile of v1, /device:TPU:0, one launch (start us, length us, event | category | flops | bytes accessed | tf_op | source)
XLA Modules:
  0.0 1815.5 jit_solution(15589106332429572018)
XLA Ops:
  26.9 37.6 %all-reduce.11 = (bf16[2048]{0:T(1024)(128)(2,1)S(1)}, bf16[1024]{0:T(1024)(128)(2,1)S(1)}, bf16[1024]{0:T(1024)(128)(2,1)S(1)}, bf16[1024]{0:T(1024)(128)(2,1)S...) all-reduce(bf16[2048]{0:T(1024)(128)(2,1)S(1)} %dynamic-update-slic, ...), channel_id=1, replica_groups=mesh['fsdp'=32] {'fsdp'}, use_global_device_ids=true, to_apply=%add.2 | all-reduce | flops 11264 | bytes 45056
  84.8 44.6 %all-gather = bf16[32,32,8]{1,2,0:T(8,128)(2,1)S(1)} all-gather(bf16[1,32,8]{1,2,0:T(8,128)(2,1)S(1)} %bitcast.252), channel_id=1, replica_groups=mesh['fsdp'=32] {'fsdp'}, dimensions={0}, use_global_device_ids=true | all-gather | bytes 16896 | tf_op jit(solution)/shard_map/all_gather | solution.py:359
  166.1 14.6 fusion
  268.1 53.1 %multiply_convert_fusion.3 = (bf16[576,4096]{1,0:T(8,128)(2,1)}, f32[576,4096]{1,0:T(8,128)}, bf16[576,4096]{1,0:T(8,128)(2,1)}, f32[576,4096]{1,0:T(8,128)}, f32[576,4096]{1,0:T(8,128)}) fusion(f32[4096]{0:T(1024)S(1)} %copy-done.107, f32[576,4096]{1,0:T(8,128)S(1)} %fusion.128, bf16[1024,4096]{1,0:T(8,128)(2,1)S(1)} %copy-done.134, ...), kind=kOutput, calls=%fused_computation.35 | convolution fusion | flops 5146214400 | bytes 57963008 | tf_op jit(solution)/shard_map/while/body/eval_jaxpr/dot_general | solution.py:35
  340.5 17.0 all-gather.15.cloned.1.call-done
  406.8 17.2 convert_reduce_fusion.1
  424.0 13.0 fusion.124
  449.3 17.3 convert_reduce_fusion
  466.7 14.1 multiply_reduce_fusion.4
  501.9 16.8 multiply_reduce_fusion
  518.7 20.3 %multiply_convert_fusion = bf16[16,576,576]{1,2,0:T(8,128)(2,1)} fusion(f32[16,576,576]{1,2,0:T(8,128)} %get-tuple-element.662, f32[16,576,576]{1,2,0:T(8,128)} %get-tuple-element.598, f32[16,576]{1,0:T(8,128)S(1)} %get-tuple-element.661, f32[16,576]{1,0:T(8,128)S(1)} %copy-done.56, pred[576]{0:T(1024)(128)(4,1)S(1)} %copy-done.102), kind=kLoop, calls=%fused_computation | loop fusion | flops 31850496 | bytes 53158464 | tf_op jit(solution)/shard_map/while/body/eval_jaxpr/convert_element_type | solution.py:220
  573.7 16.2 multiply_reduce_fusion.1
  589.9 20.7 %multiply_convert_fusion.1 = bf16[16,576,576]{1,2,0:T(8,128)(2,1)} fusion(f32[16,576,576]{1,2,0:T(8,128)} %get-tuple-element.660, f32[16,576,576]{1,2,0:T(8,128)} %get-tuple-element.600, f32[16,576]{1,0:T(8,128)S(1)} %get-tuple-element.659, f32[16,576]{1,0:T(8,128)S(1)} %copy-done.54, pred[576]{0:T(1024)(128)(4,1)S(1)} %copy-done.100), kind=kLoop, calls=%fused_computation.2 | loop fusion | flops 31850496 | bytes 53158464 | tf_op jit(solution)/shard_map/while/body/eval_jaxpr/convert_element_type | solution.py:220
  652.2 15.2 convolution_add_fusion
  667.5 12.4 reshape.578
  679.9 15.0 convolution_add_fusion.1
  695.0 12.4 reshape.579
  744.7 15.9 convolution_add_fusion.2
  773.4 37.1 %dynamic-update-slice.12 = f32[32,426720]{1,0:T(8,128)} dynamic-update-slice(f32[32,426720]{1,0:T(8,128)} %dynamic-update-slice.11, f32[32,98304]{1,0:T(8,128)} %reshape.576, s32[]{} %constant.673, s32[]{} %constant.675) | dynamic-update-slice | bytes 25165828
  820.8 48.1 %dynamic-update-slice.18 = f32[32,426720]{1,0:T(8,128)} dynamic-update-slice(f32[32,426720]{1,0:T(8,128)} %dynamic-update-slice.17, f32[32,131072]{1,0:T(8,128)} %reshape.578, s32[]{} %constant.673, s32[]{} %constant.681) | dynamic-update-slice | bytes 33554436
  870.5 48.2 %dynamic-update-slice.20 = f32[32,426720]{1,0:T(8,128)} dynamic-update-slice(f32[32,426720]{1,0:T(8,128)} %dynamic-update-slice.19, f32[32,131072]{1,0:T(8,128)} %reshape.579, s32[]{} %constant.673, s32[]{} %constant.683) | dynamic-update-slice | bytes 33554436
  923.0 14.3 dynamic-update-slice.24
  940.6 77.3 %reshape.582 = f32[13655040]{0:T(1024)} reshape(f32[32,426720]{1,0:T(8,128)} %dynamic-update-slice.26) | data formatting | bytes 109240320 | tf_op jit(solution)/shard_map/reshape | solution.py:405
  1028.1 767.0 %all-reduce.14.cloned.1.call-done = f32[13655040]{0:T(1024)} async-done(((f32[13655040]{0:T(1024)}), f32[13655040]{0:T(1024)}) %all-reduce.14.cloned.1.call-update) | async-done | bytes 54620176
  (531 shorter events, 432.9 us)
Async XLA Ops:
  7.2 60.0 %copy-start.4 = (bf16[2,1,576,1024]{3,2,1,0:T(8,128)(2,1)S(1)}, bf16[2,1,576,1024]{3,2,1,0:T(8,128)(2,1)}, u32[]{:S(2)}) copy-start(bf16[2,1,576,1024]{3,2,1,0:T(8,128)(2,1)} %param.22) | copy-start | bytes 7077892
  7.2 126.7 %all-gather.7.cloned.1.call-start = ((), (), s32[]{:S(2)}) async-start(), calls=%async_computation | async-start | bytes 6488064 | tf_op jit(solution)/shard_map/all_gather | solution.py:345
  7.9 202.6 %all-gather.9.cloned.1.call-start = ((), (), s32[]{:S(2)}) async-start(), calls=%async_computation.1 | async-start | bytes 2162688 | tf_op jit(solution)/shard_map/all_gather | solution.py:347
  8.7 247.2 %all-gather.11.cloned.1.call-start = ((), (), s32[]{:S(2)}) async-start(), calls=%async_computation.2 | async-start | bytes 8650752 | tf_op jit(solution)/shard_map/all_gather | solution.py:351
  9.4 311.7 %all-gather.13.cloned.1.call-start = ((), (), s32[]{:S(2)}) async-start(), calls=%async_computation.3 | async-start | bytes 8650752 | tf_op jit(solution)/shard_map/all_gather | solution.py:353
  10.0 347.4 %all-gather.15.cloned.1.call-start = ((), (), s32[]{:S(2)}) async-start(), calls=%async_computation.4 | async-start | bytes 2162688 | tf_op jit(solution)/shard_map/all_gather | solution.py:357
  10.0 60.0 %collective-permute-start = (bf16[128]{0:T(256)(128)(2,1)}, bf16[128]{0:T(256)(128)(2,1)S(1)}, u32[]{:S(2)}, u32[]{:S(2)}) collective-permute-start(bf16[128]{0:T(256)(128)(2,1)} %param.34), channel_id=1, source_target_pairs={{0,31},{1,0},{2,1},{3,2},{4,3},{5,4},{6,5},{7,6},{8,7},{9,8},{10,9... | collective-permute-start | bytes 776 | tf_op jit(solution)/shard_map/ppermute | solution.py:330
  16.5 1778.7 %all-reduce.14.cloned.1.call-start = ((), (), s32[]{:S(2)}) async-start(), calls=%async_computation.5 | async-start | bytes 109240320
  67.2 66.7 %copy-start.66 = (f32[576]{0:T(1024)}, f32[576]{0:T(1024)S(1)}, u32[]{:S(2)}) copy-start(f32[576]{0:T(1024)S(1)} %get-tuple-element.680) | copy-start | bytes 6916
  67.2 77.5 %copy-start.68 = (f32[576]{0:T(1024)}, f32[576]{0:T(1024)S(1)}, u32[]{:S(2)}) copy-start(f32[576]{0:T(1024)S(1)} %get-tuple-element.681) | copy-start | bytes 6916
  68.0 63.8 %copy-start.82 = (f32[576]{0:T(1024)}, f32[576]{0:T(1024)S(1)}, u32[]{:S(2)}) copy-start(f32[576]{0:T(1024)S(1)} %get-tuple-element.475) | copy-start | bytes 6916
  68.0 63.8 %copy-start.84 = (f32[576]{0:T(1024)}, f32[576]{0:T(1024)S(1)}, u32[]{:S(2)}) copy-start(f32[576]{0:T(1024)S(1)} %get-tuple-element.474) | copy-start | bytes 6916
  68.0 76.6 %copy-start.78 = (f32[576]{0:T(1024)}, f32[576]{0:T(1024)S(1)}, u32[]{:S(2)}) copy-start(f32[576]{0:T(1024)S(1)} %fusion.95) | copy-start | bytes 6916
  68.0 65.8 %copy-start.76 = (f32[576]{0:T(1024)}, f32[576]{0:T(1024)S(1)}, u32[]{:S(2)}) copy-start(f32[576]{0:T(1024)S(1)} %fusion.98) | copy-start | bytes 6916
  70.1 5.1 collective-permute-start.1
  75.1 3.9 collective-permute-start.2
  79.1 5.0 collective-permute-start.3
  84.1 49.0 %collective-permute-start.4 = (bf16[2048]{0:T(1024)(128)(2,1)S(1)}, bf16[2048]{0:T(1024)(128)(2,1)S(1)}, u32[]{:S(2)}, u32[]{:S(2)}) collective-permute-start(bf16[2048]{0:T(1024)(128)(2,1)S(1)} %get-tuple-element.593), channel_id=1, source_target_pairs={{0,16},{1,17},{2,18},{3,19},{4,20},{5,21},{6,22},{7,23},{8,24},{9,... | collective-permute-start | bytes 12296 | tf_op jit(solution)/shard_map/ppermute | solution.py:330
  130.0 293.9 %copy-start.57 = (f32[1024]{0:T(1024)}, f32[1024]{0:T(1024)S(1)}, u32[]{:S(2)}) copy-start(f32[1024]{0:T(1024)S(1)} %convert_element_type.382) | copy-start | bytes 12292
  268.1 53.1 %copy-start.131 = (f32[1024]{0:T(1024)S(1)}, f32[1024]{0:T(1024)}, u32[]{:S(2)}) copy-start(f32[1024]{0:T(1024)} %convert_element_type.386) | copy-start | bytes 12292
  330.9 61.2 %copy-start.6 = (f32[576,1024]{1,0:T(8,128)}, f32[576,1024]{1,0:T(8,128)S(1)}, u32[]{:S(2)}) copy-start(f32[576,1024]{1,0:T(8,128)S(1)} %get-tuple-element.653) | copy-start | bytes 7077892
  338.6 53.4 %copy-start.94 = (f32[576]{0:T(1024)}, f32[576]{0:T(1024)S(1)}, u32[]{:S(2)}) copy-start(f32[576]{0:T(1024)S(1)} %broadcast_multiply_fusion) | copy-start | bytes 6916
  377.4 59.6 %copy-start.61 = (f32[576,8]{0,1:T(8,128)}, f32[576,8]{0,1:T(8,128)S(1)}, u32[]{:S(2)}) copy-start(f32[576,8]{0,1:T(8,128)S(1)} %fusion.65) | copy-start | bytes 55300
  396.4 160.1 %copy-start.14 = (f32[576,1024]{1,0:T(8,128)}, f32[576,1024]{1,0:T(8,128)S(1)}, u32[]{:S(2)}) copy-start(f32[576,1024]{1,0:T(8,128)S(1)} %add_add_fusion.9) | copy-start | bytes 7077892
  (136 other events, 1210.9 us)
Sparse Core Ops, SparseCore 0:
  10.9 73.0 all-gather.6
  86.9 54.8 all-gather.8
  144.6 76.2 all-gather.10
  223.6 76.0 all-gather.12
  302.4 54.9 all-gather.14
  1018.0 777.1 all-reduce.13
